TPU v7x, 128 devices: a whole 4x4x4 slice. The times are simulated.
128 devices in a mesh: layer: 4 (over z), row: 32 (over y, x, core).
Axes of the slice: x: 4, y: 4, z: 4, core: 2. Of those that a mesh axis runs over, the one named last changes fastest.
Arguments:
- rhs_sub: float32 [4, 3, 4096, 256], P('layer', None, 'row'), may hold values from -6 to 6
- rhs_root: float32 [2048, 256], P('row'), may hold values from -6 to 6
- lower_inv: float32 [4, 3, 4096, 4096], P('layer', None, 'row'), may hold values from -0.09375 to 0.09375
- upper_inv: float32 [4, 3, 4096, 4096], P('layer', None, 'row'), may hold values from -0.09375 to 0.09375
- coupling_low: float32 [4, 3, 2048, 4096], P('layer', None, None, 'row'), may hold values from -0.0390625 to 0.0390625
- coupling_up: float32 [4, 3, 4096, 2048], P('layer', None, 'row'), may hold values from -0.1875 to 0.1875
- tile_mask: int32 [4, 3, 16, 32], P('layer', None, None, 'row'), may hold values 0 or 1
- root_inv: float32 [2048, 2048], P('row'), may hold values from -0.125 to 0.125
Outputs:
- sol_sub: float32 [4, 3, 4096, 256], P('layer', None, 'row')
- sol_root: float32 [2048, 256], P('row')
All inputs are finite; a program needn't handle non-finite values. No bound on the sum of `tile_mask` on one device may be relied on, other than what follows from the above.
Results may differ from a plain program's by a relative error of at most 0.0001.
Values sent between devices are 32-bit elements; how exact they have to be, the bound alone decides.
No kernel may reach another device: no remote copies, remote signals or barrier semaphores. Data moves between devices by JAX's collectives and lax.ppermute only.
A program may use at most 128 MiB of HBM per device.

v0:
```python
import jax
import jax.numpy as jnp
from jax import lax
from jax.sharding import PartitionSpec as P

TILE = 128


def masked_tiles(coupling, pattern, tile, flipped):
    blocks, height, breadth = coupling.shape
    shaped = coupling.reshape(blocks, height // tile, tile, breadth // tile, tile)
    if flipped:
        pattern = jnp.transpose(pattern, (0, 2, 1))
    weights = pattern.astype(jnp.float32)[:, :, None, :, None]
    return (shaped * weights).reshape(blocks, height, breadth)


def fold_single(matrix, piece):
    return jnp.dot(
        matrix, piece, precision=lax.Precision.HIGHEST, preferred_element_type=jnp.float32
    )


def body(rhs_sub, rhs_root, lower_inv, upper_inv, coupling_low, coupling_up, tile_mask, root_inv):
    highest = lax.Precision.HIGHEST
    lower = lower_inv[0]
    upper = upper_inv[0]
    vectors = rhs_sub[0]
    blocks = vectors.shape[0]
    results = []
    for index in range(blocks):
        results.append(
            fold_single(lower[index], lax.all_gather(vectors[index], "row", axis=0, tiled=True))
        )
    interim = jnp.stack(results)
    lower_coupling = masked_tiles(coupling_low[0], tile_mask[0], TILE, False)
    local_part = lax.psum_scatter(
        jnp.einsum("kas,ksr->ar", lower_coupling, interim, precision=highest),
        "row",
        scatter_dimension=0,
        tiled=True,
    )
    layer_total = lax.psum(local_part, "layer")
    reduced = rhs_root - layer_total
    columns = root_inv
    sol_root = jnp.dot(
        columns,
        lax.all_gather(reduced, "row", axis=0, tiled=True),
        precision=highest,
        preferred_element_type=jnp.float32,
    )
    upper_coupling = masked_tiles(coupling_up[0], tile_mask[0], TILE, True)
    columns = upper_coupling
    coupled = jnp.einsum(
        "ksa,ar->ksr",
        columns,
        lax.all_gather(sol_root, "row", axis=0, tiled=True),
        precision=highest,
    )
    residue = interim - coupled
    outputs = []
    for index in range(blocks):
        outputs.append(
            fold_single(upper[index], lax.all_gather(residue[index], "row", axis=0, tiled=True))
        )
    solved = jnp.stack(outputs)
    return (solved[None], sol_root)


def solution(mesh):
    return jax.shard_map(
        body,
        mesh=mesh,
        in_specs=(
            P("layer", None, "row", None),
            P("row", None),
            P("layer", None, "row", None),
            P("layer", None, "row", None),
            P("layer", None, None, "row"),
            P("layer", None, "row", None),
            P("layer", None, None, "row"),
            P("row", None),
        ),
        out_specs=(P("layer", None, "row", None), P("row", None)),
        check_vma=False,
    )
```

profile of v0, /device:TPU:1, one launch (start us, length us, event | category | flops | bytes accessed | tf_op | source)
XLA Modules:
  0.0 543.6 jit_solution(12536181070227293686)
XLA Ops:
  7.2 0.0 copy-start
  7.2 0.0 all-gather.19.cloned.1.call-start
  7.2 1.8 fusion.65
  9.1 0.0 all-gather.19.cloned.1.call-update
  9.1 0.0 all-gather.23.cloned.1.call-start
  9.1 0.7 all-gather.23.cloned.1.call-update
  9.8 0.0 all-gather.21.cloned.1.call-start
  9.9 0.7 all-gather.21.cloned.1.call-update
  10.6 0.0 reduce-scatter.2.cloned.1.call-start
  10.6 0.7 convert_element_type.19
  11.3 0.1 broadcast_bitcast_fusion
  11.4 48.9 %all-gather.19.cloned.1.call-done = f32[1,1,4096,256]{3,2,1,0:T(8,128)} async-done(((f32[1,1,128,256]{3,2,1,0:T(8,128)}), f32[1,1,4096,256]{3,2,1,0:T(8,128)}) %all-gather.19.cloned.1.call-update) | async-done | bytes 4194320 | tf_op jit(solution)/shard_map/all_gather | solution.py:33
  60.3 4.9 fusion.33
  65.3 42.7 %all-gather.23.cloned.1.call-done = f32[1,1,4096,256]{3,2,1,0:T(8,128)} async-done(((f32[1,1,128,256]{3,2,1,0:T(8,128)}), f32[1,1,4096,256]{3,2,1,0:T(8,128)}) %all-gather.23.cloned.1.call-update) | async-done | bytes 4194320 | tf_op jit(solution)/shard_map/all_gather | solution.py:33
  108.0 4.9 fusion.43
  112.9 42.7 %all-gather.21.cloned.1.call-done = f32[1,1,4096,256]{3,2,1,0:T(8,128)} async-done(((f32[1,1,128,256]{3,2,1,0:T(8,128)}), f32[1,1,4096,256]{3,2,1,0:T(8,128)}) %all-gather.21.cloned.1.call-update) | async-done | bytes 4194320 | tf_op jit(solution)/shard_map/all_gather | solution.py:33
  155.6 5.1 fusion.38
  160.6 0.0 copy-start.2
  160.7 5.1 fusion.14
  165.8 0.0 reduce-scatter.2.cloned.1.call-update
  165.8 0.0 all-reduce.2.cloned.1.call-start
  165.8 76.2 %reduce-scatter.2.cloned.1.call-done = f32[64,256]{1,0:T(8,128)} async-done(((f32[2048,256]{1,0:T(8,128)}), f32[64,256]{1,0:T(8,128)}) %reduce-scatter.2.cloned.1.call-update) | async-done | bytes 65552 | tf_op jit(solution)/shard_map/reduce_scatter | solution.py:37
  242.1 0.0 all-reduce.2.cloned.1.call-update
  242.1 0.0 all-gather.15.cloned.1.call-start
  242.1 42.6 %all-reduce.2.cloned.1.call-done = f32[64,256]{1,0:T(8,128)} async-done(((f32[64,256]{1,0:T(8,128)}), f32[64,256]{1,0:T(8,128)}) %all-reduce.2.cloned.1.call-update) | async-done | bytes 65552 | tf_op jit(solution)/shard_map/psum | solution.py:43
  284.8 1.5 sub.6
  286.3 0.0 all-gather.15.cloned.1.call-update
  286.3 0.2 all-gather.17.cloned.1.call-start
  286.5 47.1 %all-gather.15.cloned.1.call-done = f32[2048,256]{1,0:T(8,128)} async-done(((f32[64,256]{1,0:T(8,128)}), f32[2048,256]{1,0:T(8,128)}) %all-gather.15.cloned.1.call-update) | async-done | bytes 2097168 | tf_op jit(solution)/shard_map/all_gather | solution.py:48
  333.6 0.0 copy-done
  333.6 3.6 convolution_bitcast_fusion
  337.1 0.0 all-gather.17.cloned.1.call-update
  337.2 0.0 all-gather.25.cloned.1.call-start
  337.2 42.9 %all-gather.17.cloned.1.call-done = f32[2048,256]{1,0:T(8,128)} async-done(((f32[64,256]{1,0:T(8,128)}), f32[2048,256]{1,0:T(8,128)}) %all-gather.17.cloned.1.call-update) | async-done | bytes 2097168 | tf_op jit(solution)/shard_map/all_gather | solution.py:57
  380.1 5.3 fusion.30
  385.4 0.8 fusion.64
  386.1 0.0 all-gather.25.cloned.1.call-update
  386.1 0.0 all-gather.29.cloned.1.call-start
  386.2 0.7 all-gather.29.cloned.1.call-update
  386.9 0.0 all-gather.27.cloned.1.call-start
  386.9 0.5 all-gather.27.cloned.1.call-update
  387.5 44.1 %all-gather.25.cloned.1.call-done = f32[1,4096,256]{2,1,0:T(8,128)} async-done(((f32[1,128,256]{2,1,0:T(8,128)}), f32[1,4096,256]{2,1,0:T(8,128)}) %all-gather.25.cloned.1.call-update) | async-done | bytes 4194320 | tf_op jit(solution)/shard_map/all_gather | solution.py:64
  431.5 9.2 %fusion.48 = f32[1,128,256]{1,2,0:T(8,128)S(1)} fusion(f32[1,3,128,4096]{3,2,1,0:T(8,128)} %param.11, f32[1,4096,256]{2,1,0:T(8,128)} %all-gather.25.cloned.1.call-done), kind=kOutput, calls=%fused_computation.36 | convolution fusion | flops 1610612736 | bytes 6422528 | tf_op jit(solution)/shard_map/dot_general | solution.py:19
  440.7 38.4 %all-gather.29.cloned.1.call-done = f32[1,4096,256]{2,1,0:T(8,128)} async-done(((f32[1,128,256]{2,1,0:T(8,128)}), f32[1,4096,256]{2,1,0:T(8,128)}) %all-gather.29.cloned.1.call-update) | async-done | bytes 4194320 | tf_op jit(solution)/shard_map/all_gather | solution.py:64
  479.2 9.2 %fusion.58 = f32[1,128,256]{1,2,0:T(8,128)S(1)} fusion(f32[1,3,128,4096]{3,2,1,0:T(8,128)} %param.11, f32[1,4096,256]{2,1,0:T(8,128)} %all-gather.29.cloned.1.call-done), kind=kOutput, calls=%fused_computation.38 | convolution fusion | flops 1610612736 | bytes 6422528 | tf_op jit(solution)/shard_map/dot_general | solution.py:19
  488.4 38.3 %all-gather.27.cloned.1.call-done = f32[1,4096,256]{2,1,0:T(8,128)} async-done(((f32[1,128,256]{2,1,0:T(8,128)}), f32[1,4096,256]{2,1,0:T(8,128)}) %all-gather.27.cloned.1.call-update) | async-done | bytes 4194320 | tf_op jit(solution)/shard_map/all_gather | solution.py:64
  526.6 9.2 %fusion.53 = f32[1,128,256]{1,2,0:T(8,128)S(1)} fusion(f32[1,3,128,4096]{3,2,1,0:T(8,128)} %param.11, f32[1,4096,256]{2,1,0:T(8,128)} %all-gather.27.cloned.1.call-done), kind=kOutput, calls=%fused_computation.37 | convolution fusion | flops 1610612736 | bytes 6422528 | tf_op jit(solution)/shard_map/dot_general | solution.py:19
  535.9 0.9 copy.10
  (6 shorter events, 0.1 us)
Async XLA Ops:
  7.2 326.4 %copy-start = (f32[64,2048]{1,0:T(8,128)S(1)}, f32[64,2048]{1,0:T(8,128)}, u32[]{:S(2)}) copy-start(f32[64,2048]{1,0:T(8,128)} %param.15) | copy-start | bytes 1572868
  7.2 53.2 %all-gather.19.cloned.1.call-start = ((), (), s32[]{:S(2)}) async-start(), calls=%async_computation.5 | async-start | bytes 4325376 | tf_op jit(solution)/shard_map/all_gather | solution.py:33
  9.1 98.9 %all-gather.23.cloned.1.call-start = ((), (), s32[]{:S(2)}) async-start(), calls=%async_computation.7 | async-start | bytes 4325376 | tf_op jit(solution)/shard_map/all_gather | solution.py:33
  9.8 145.7 %all-gather.21.cloned.1.call-start = ((), (), s32[]{:S(2)}) async-start(), calls=%async_computation.6 | async-start | bytes 4325376 | tf_op jit(solution)/shard_map/all_gather | solution.py:33
  10.6 231.5 %reduce-scatter.2.cloned.1.call-start = ((), (), s32[]{:S(2)}) async-start(), calls=%async_computation.1 | async-start | bytes 2162688 | tf_op jit(solution)/shard_map/reduce_scatter | solution.py:37
  155.6 5.1 copy-start.1
  160.6 124.1 %copy-start.2 = (f32[64,256]{1,0:T(8,128)S(1)}, f32[64,256]{1,0:T(8,128)}, u32[]{:S(2)}) copy-start(f32[64,256]{1,0:T(8,128)} %param.9) | copy-start | bytes 196612
  165.8 119.0 %all-reduce.2.cloned.1.call-start = ((), (), s32[]{:S(2)}) async-start(), calls=%async_computation.2 | async-start | bytes 131072 | tf_op jit(solution)/shard_map/psum | solution.py:43
  242.1 91.5 %all-gather.15.cloned.1.call-start = ((), (), s32[]{:S(2)}) async-start(), calls=%async_computation.3 | async-start | bytes 2162688 | tf_op jit(solution)/shard_map/all_gather | solution.py:48
  286.3 93.8 %all-gather.17.cloned.1.call-start = ((), (), s32[]{:S(2)}) async-start(), calls=%async_computation.4 | async-start | bytes 2162688 | tf_op jit(solution)/shard_map/all_gather | solution.py:57
  337.2 94.4 %all-gather.25.cloned.1.call-start = ((), (), s32[]{:S(2)}) async-start(), calls=%async_computation.8 | async-start | bytes 4325376 | tf_op jit(solution)/shard_map/all_gather | solution.py:64
  386.1 93.0 %all-gather.29.cloned.1.call-start = ((), (), s32[]{:S(2)}) async-start(), calls=%async_computation.10 | async-start | bytes 4325376 | tf_op jit(solution)/shard_map/all_gather | solution.py:64
  386.9 139.8 %all-gather.27.cloned.1.call-start = ((), (), s32[]{:S(2)}) async-start(), calls=%async_computation.9 | async-start | bytes 4325376 | tf_op jit(solution)/shard_map/all_gather | solution.py:64
Sparse Core Ops, SparseCore 0:
  10.8 49.4 all-gather.18
  62.6 45.3 all-gather.22
  110.2 45.3 all-gather.20
  165.9 76.1 reduce-scatter.1
  244.2 40.5 all-reduce.1
  287.5 46.0 all-gather.14
  337.3 42.7 all-gather.16
  386.3 45.2 all-gather.24
  433.8 45.3 all-gather.28
  481.3 45.3 all-gather.26
where the time goes:
time: 544 us
  waiting for transfers between devices  467 us (86%)
  matrix products  56.3 us (10%)
  between operations  14.3 us (3%)
    all_gather x3, waiting for transfers between devices, body(): lax.all_gather(vectors[index], 'row', axis=0, tiled=True)  134 us
    all_gather x3, waiting for transfers between devices, body(): lax.all_gather(residue[index], 'row', axis=0, tiled=True)  121 us
    reduce_scatter x1, waiting for transfers between devices, body(): lax.psum_scatter(jnp.einsum('kas,ksr->ar', lower_coupling, interim, preci...  76.2 us
    all_gather x1, waiting for transfers between devices, body(): lax.all_gather(reduced, 'row', axis=0, tiled=True)  47.1 us
    all_gather x1, waiting for transfers between devices, body(): lax.all_gather(sol_root, 'row', axis=0, tiled=True)  42.9 us
    psum x1, waiting for transfers between devices, body(): layer_total = lax.psum(local_part, 'layer')  42.6 us
    dot_general x6, matrix products, fold_single(): jnp.dot(matrix, piece, precision=lax.Precision.HIGHEST, preferred_element...  42.4 us
  transfers between devices with their start and end apart: 10, of which 10 were waited for; matrix products, arithmetic and copies ran while one was open for 5% of the time, Pallas kernels for 0%

commit v1 on v0

--- a/solution.py
+++ b/solution.py
@@ -61,7 +61,13 @@
     outputs = []
     for index in range(blocks):
         outputs.append(
-            fold_single(upper[index], lax.all_gather(residue[index], "row", axis=0, tiled=True))
+            fold_single(
+                upper[index],
+                jnp.concatenate(
+                    lax.all_to_all(jnp.stack([residue[index]] * lax.axis_size("row")), "row", 0, 0),
+                    axis=0,
+                ),
+            )
         )
     solved = jnp.stack(outputs)
     return (solved[None], sol_root)

time: 544 us -> 575 us (1.057)
  blocking collectives: 0 us -> 111 us
  waiting for transfers between devices: 467 us -> 378 us
    all_gather x3 -> x0, waiting for transfers between devices: 121 us -> none  [body(): lax.all_gather(residue[index], 'row', axis=0, tiled=True)]
    all_to_all x0 -> x2, blocking collectives: none -> 111 us  [body(): lax.all_to_all(jnp.stack([residue[index]] * lax.axis_size('row')), 'row',...]
    all_to_all x0 -> x1, waiting for transfers between devices: none -> 32.9 us  [body(): lax.all_to_all(jnp.stack([residue[index]] * lax.axis_size('row')), 'row',...]
  transfers between devices with their start and end apart: 10 -> 8, of which waited for: 10 -> 8; matrix products, arithmetic and copies ran while one was open for 5% -> 5% of each run, Pallas kernels for 0% -> 0%
where the time goes in v1:
time: 575 us; the launch traced here: 572 us
  waiting for transfers between devices  378 us (66%)
  blocking collectives  111 us (19%)
  matrix products  55.7 us (10%)
  between operations  14.3 us (2%)
  local copies, waits for them, and re-layouts  6.26 us (1%)
    all_gather x3, waiting for transfers between devices, body(): lax.all_gather(vectors[index], 'row', axis=0, tiled=True)  134 us
    all_to_all x2, blocking collectives, body(): lax.all_to_all(jnp.stack([residue[index]] * lax.axis_size('row')), 'row',...  111 us
    reduce_scatter x1, waiting for transfers between devices, body(): lax.psum_scatter(jnp.einsum('kas,ksr->ar', lower_coupling, interim, preci...  76.2 us
    all_gather x1, waiting for transfers between devices, body(): lax.all_gather(reduced, 'row', axis=0, tiled=True)  47.1 us
    all_gather x1, waiting for transfers between devices, body(): lax.all_gather(sol_root, 'row', axis=0, tiled=True)  42.9 us
    psum x1, waiting for transfers between devices, body(): layer_total = lax.psum(local_part, 'layer')  42.6 us
    dot_general x6, matrix products, fold_single(): jnp.dot(matrix, piece, precision=lax.Precision.HIGHEST, preferred_element...  41.8 us
    all_to_all x1, waiting for transfers between devices, body(): lax.all_to_all(jnp.stack([residue[index]] * lax.axis_size('row')), 'row',...  32.9 us
  transfers between devices with their start and end apart: 8, of which 8 were waited for; matrix products, arithmetic and copies ran while one was open for 5% of the time, Pallas kernels for 0%

profile of v1, /device:TPU:1, one launch (start us, length us, event | category | flops | bytes accessed | tf_op | source)
XLA Modules:
  0.0 571.8 jit_solution(9698089775046689618)
XLA Ops:
  7.2 0.0 copy-start
  7.2 0.0 all-gather.13.cloned.1.call-start
  7.2 1.8 fusion.55
  9.0 0.0 all-gather.13.cloned.1.call-update
  9.1 0.0 all-gather.17.cloned.1.call-start
  9.1 0.7 all-gather.17.cloned.1.call-update
  9.8 0.0 all-gather.15.cloned.1.call-start
  9.9 0.7 all-gather.15.cloned.1.call-update
  10.6 0.0 reduce-scatter.2.cloned.1.call-start
  10.6 0.7 convert_element_type.19
  11.3 0.1 broadcast_bitcast_fusion
  11.4 48.9 %all-gather.13.cloned.1.call-done = f32[1,1,4096,256]{3,2,1,0:T(8,128)} async-done(((f32[1,1,128,256]{3,2,1,0:T(8,128)}), f32[1,1,4096,256]{3,2,1,0:T(8,128)}) %all-gather.13.cloned.1.call-update) | async-done | bytes 4194320 | tf_op jit(solution)/shard_map/all_gather | solution.py:33
  60.3 4.9 fusion.39
  65.3 42.7 %all-gather.17.cloned.1.call-done = f32[1,1,4096,256]{3,2,1,0:T(8,128)} async-done(((f32[1,1,128,256]{3,2,1,0:T(8,128)}), f32[1,1,4096,256]{3,2,1,0:T(8,128)}) %all-gather.17.cloned.1.call-update) | async-done | bytes 4194320 | tf_op jit(solution)/shard_map/all_gather | solution.py:33
  108.0 4.9 fusion.49
  112.9 42.7 %all-gather.15.cloned.1.call-done = f32[1,1,4096,256]{3,2,1,0:T(8,128)} async-done(((f32[1,1,128,256]{3,2,1,0:T(8,128)}), f32[1,1,4096,256]{3,2,1,0:T(8,128)}) %all-gather.15.cloned.1.call-update) | async-done | bytes 4194320 | tf_op jit(solution)/shard_map/all_gather | solution.py:33
  155.6 5.1 fusion.44
  160.6 0.0 copy-start.3
  160.7 0.0 copy-done.2
  160.7 5.1 fusion.8
  165.7 0.0 reduce-scatter.2.cloned.1.call-update
  165.8 0.0 all-reduce.2.cloned.1.call-start
  165.8 76.2 %reduce-scatter.2.cloned.1.call-done = f32[64,256]{1,0:T(8,128)} async-done(((f32[2048,256]{1,0:T(8,128)}), f32[64,256]{1,0:T(8,128)}) %reduce-scatter.2.cloned.1.call-update) | async-done | bytes 65552 | tf_op jit(solution)/shard_map/reduce_scatter | solution.py:37
  242.0 0.0 all-reduce.2.cloned.1.call-update
  242.1 0.0 all-gather.9.cloned.1.call-start
  242.1 42.6 %all-reduce.2.cloned.1.call-done = f32[64,256]{1,0:T(8,128)} async-done(((f32[64,256]{1,0:T(8,128)}), f32[64,256]{1,0:T(8,128)}) %all-reduce.2.cloned.1.call-update) | async-done | bytes 65552 | tf_op jit(solution)/shard_map/psum | solution.py:43
  284.8 0.0 copy-done.3
  284.8 1.5 sub.6
  286.2 0.0 all-gather.9.cloned.1.call-update
  286.3 0.2 all-gather.11.cloned.1.call-start
  286.5 47.1 %all-gather.9.cloned.1.call-done = f32[2048,256]{1,0:T(8,128)} async-done(((f32[64,256]{1,0:T(8,128)}), f32[2048,256]{1,0:T(8,128)}) %all-gather.9.cloned.1.call-update) | async-done | bytes 2097168 | tf_op jit(solution)/shard_map/all_gather | solution.py:48
  333.6 0.0 copy-done
  333.6 3.6 convolution_bitcast_fusion
  337.1 0.0 all-gather.11.cloned.1.call-update
  337.1 42.9 %all-gather.11.cloned.1.call-done = f32[2048,256]{1,0:T(8,128)} async-done(((f32[64,256]{1,0:T(8,128)}), f32[2048,256]{1,0:T(8,128)}) %all-gather.11.cloned.1.call-update) | async-done | bytes 2097168 | tf_op jit(solution)/shard_map/all_gather | solution.py:57
  380.1 5.3 fusion.27
  385.4 0.5 stack.37
  385.9 55.9 %all_to_all.15 = f32[32,128,256]{2,1,0:T(8,128)} all-to-all(f32[32,128,256]{2,1,0:T(8,128)S(1)} %stack.37), channel_id=1, replica_groups=mesh['layer'=4,'row'=32] {'row'}, dimensions={0} | all-to-all | bytes 8388608 | tf_op jit(solution)/shard_map/all_to_all | solution.py:67
  441.8 0.5 stack.41
  442.2 54.6 %all_to_all.16 = f32[32,128,256]{2,1,0:T(8,128)} all-to-all(f32[32,128,256]{2,1,0:T(8,128)S(1)} %stack.41), channel_id=1, replica_groups=mesh['layer'=4,'row'=32] {'row'}, dimensions={0} | all-to-all | bytes 8388608 | tf_op jit(solution)/shard_map/all_to_all | solution.py:67
  496.9 2.5 stack.39
  499.3 4.9 all-to-all-start.1
  504.2 0.0 copy-start.1
  504.2 9.3 %fusion.30 = f32[1,128,256]{1,2,0:T(8,128)S(1)} fusion(f32[4096,256]{1,0:T(8,128)} %bitcast.106, f32[1,3,128,4096]{3,2,1,0:T(8,128)} %param.11), kind=kOutput, calls=%fused_computation.30 | convolution fusion | flops 1610612736 | bytes 6422528 | tf_op jit(solution)/shard_map/dot_general | solution.py:19
  513.6 8.4 %fusion.36 = f32[1,128,256]{1,2,0:T(8,128)S(1)} fusion(f32[4096,256]{1,0:T(8,128)S(1)} %bitcast.107, f32[1,3,128,4096]{3,2,1,0:T(8,128)} %param.11), kind=kOutput, calls=%fused_computation.32 | convolution fusion | flops 1610612736 | bytes 6422528 | tf_op jit(solution)/shard_map/dot_general | solution.py:19
  521.9 32.9 %all-to-all-done.1 = f32[32,128,256]{2,1,0:T(8,128)} async-done(((f32[32,128,256]{2,1,0:T(8,128)}), f32[32,128,256]{2,1,0:T(8,128)}, u32[]{:S(2)}, u32[]{:S(2)}) %all-to-all-start.1) | async-done | bytes 4194336 | tf_op jit(solution)/shard_map/all_to_all | solution.py:67
  554.8 9.2 %fusion.33 = f32[1,128,256]{1,2,0:T(8,128)S(1)} fusion(f32[4096,256]{1,0:T(8,128)} %bitcast.20, f32[1,3,128,4096]{3,2,1,0:T(8,128)} %param.11), kind=kOutput, calls=%fused_computation.31 | convolution fusion | flops 1610612736 | bytes 6422528 | tf_op jit(solution)/shard_map/dot_general | solution.py:19
  564.1 0.9 copy.10
  (6 shorter events, 0.1 us)
Async XLA Ops:
  7.2 326.4 %copy-start = (f32[64,2048]{1,0:T(8,128)S(1)}, f32[64,2048]{1,0:T(8,128)}, u32[]{:S(2)}) copy-start(f32[64,2048]{1,0:T(8,128)} %param.15) | copy-start | bytes 1572868
  7.2 53.2 %all-gather.13.cloned.1.call-start = ((), (), s32[]{:S(2)}) async-start(), calls=%async_computation.8 | async-start | bytes 4325376 | tf_op jit(solution)/shard_map/all_gather | solution.py:33
  9.1 98.9 %all-gather.17.cloned.1.call-start = ((), (), s32[]{:S(2)}) async-start(), calls=%async_computation.10 | async-start | bytes 4325376 | tf_op jit(solution)/shard_map/all_gather | solution.py:33
  9.8 145.7 %all-gather.15.cloned.1.call-start = ((), (), s32[]{:S(2)}) async-start(), calls=%async_computation.9 | async-start | bytes 4325376 | tf_op jit(solution)/shard_map/all_gather | solution.py:33
  10.6 231.5 %reduce-scatter.2.cloned.1.call-start = ((), (), s32[]{:S(2)}) async-start(), calls=%async_computation.4 | async-start | bytes 2162688 | tf_op jit(solution)/shard_map/reduce_scatter | solution.py:37
  155.6 5.1 copy-start.2
  160.6 124.1 %copy-start.3 = (f32[64,256]{1,0:T(8,128)S(1)}, f32[64,256]{1,0:T(8,128)}, u32[]{:S(2)}) copy-start(f32[64,256]{1,0:T(8,128)} %param.9) | copy-start | bytes 196612
  165.8 119.0 %all-reduce.2.cloned.1.call-start = ((), (), s32[]{:S(2)}) async-start(), calls=%async_computation.5 | async-start | bytes 131072 | tf_op jit(solution)/shard_map/psum | solution.py:43
  242.1 91.5 %all-gather.9.cloned.1.call-start = ((), (), s32[]{:S(2)}) async-start(), calls=%async_computation.6 | async-start | bytes 2162688 | tf_op jit(solution)/shard_map/all_gather | solution.py:48
  286.3 93.8 %all-gather.11.cloned.1.call-start = ((), (), s32[]{:S(2)}) async-start(), calls=%async_computation.7 | async-start | bytes 2162688 | tf_op jit(solution)/shard_map/all_gather | solution.py:57
  499.3 55.5 %all-to-all-start.1 = ((f32[32,128,256]{2,1,0:T(8,128)}), f32[32,128,256]{2,1,0:T(8,128)}, u32[]{:S(2)}, u32[]{:S(2)}) async-start(f32[32,128,256]{2,1,0:T(8,128)} %stack.39), calls=%async_computation.2 | async-start | bytes 8388608 | tf_op jit(solution)/shard_map/all_to_all | solution.py:67
  504.2 9.4 %copy-start.1 = (f32[32,128,256]{2,1,0:T(8,128)S(1)}, f32[32,128,256]{2,1,0:T(8,128)}, u32[]{:S(2)}) copy-start(f32[32,128,256]{2,1,0:T(8,128)} %all_to_all.16) | copy-start | bytes 12582916
Sparse Core Ops, SparseCore 0:
  10.8 49.4 all-gather.12
  62.6 45.3 all-gather.16
  110.2 45.3 all-gather.14
  165.9 76.1 reduce-scatter.1
  244.2 40.5 all-reduce.1
  287.5 46.0 all-gather.8
  337.3 42.7 all-gather.10
